TPU v7x, 256 devices: a whole 4x4x8 slice. The times are simulated.
256 devices in a mesh: row: 16 (over y, x), col: 16 (over z, core).
Axes of the slice: x: 4, y: 4, z: 8, core: 2. Of those that a mesh axis runs over, the one named last changes fastest.
Arguments:
- factor_diag: float32 [2, 512, 512], replicated, as said below
- factor_mid: float32 [512, 512], replicated, may hold values from -0.25 to 0.25
- factor_low: float32 [2, 16384, 512], P(None, ('row', 'col')), may hold values from -0.046875 to 0.046875
- adjoint_diag: float32 [2, 512, 512], replicated, may hold values from -6 to 6
- adjoint_mid: float32 [512, 512], replicated, may hold values from -6 to 6
- adjoint_low: float32 [2, 16384, 512], P(None, ('row', 'col')), may hold values from -6 to 6
- trailing_adjoint: float32 [16384, 16, 1024], P('row', None, 'col'), as said below
Outputs:
- grad_diag: float32 [2, 512, 512], replicated
- grad_mid: float32 [512, 512], replicated
- grad_low: float32 [2, 16384, 512], P(None, ('row', 'col'))
Inputs may be any that keep to these rules, and one draw needn't show every extreme that they name: `factor_diag`: each of the two [512, 512] blocks is lower triangular with diagonal entries between 1 and 2. `trailing_adjoint`: symmetric when read as an 16384 x 16384 matrix in row-major order.
All inputs are finite; a program needn't handle non-finite values.
Results may differ from a plain program's by a relative error of at most 0.000065.
Values sent between devices are 32-bit elements; how exact they have to be, the bound alone decides.
No kernel may reach another device: no remote copies, remote signals or barrier semaphores. Data moves between devices by JAX's collectives and lax.ppermute only.
A program may use at most 128 MiB of HBM per device.

v0:
```python
import jax
import jax.numpy as jnp
from jax import lax
from jax.sharding import PartitionSpec as P


def lower_half(matrix):
    return jnp.tril(matrix, -1) + 0.5 * jnp.diag(jnp.diag(matrix))


def product(left_side, right_side):
    return jnp.dot(
        left_side, right_side, precision=lax.Precision.HIGHEST, preferred_element_type=jnp.float32
    )


def right_solve(factor, row_block):
    return jax.scipy.linalg.solve_triangular(factor, row_block.T, trans=1, lower=True).T


def diag_adjoint(factor, adjoint):
    inner_term = lower_half(product(factor.T, adjoint))
    halfway = jax.scipy.linalg.solve_triangular(factor, inner_term, trans=1, lower=True)
    whole_term = right_solve(factor, halfway)
    return 0.5 * (whole_term + whole_term.T)


def shards(
    factor_diag, factor_mid, factor_low, adjoint_diag, adjoint_mid, adjoint_low, trailing_adjoint
):
    block_rows, row_groups, group_cols = trailing_adjoint.shape
    local_block = trailing_adjoint.reshape(block_rows, row_groups * group_cols)

    def image_of(panel):
        columns = lax.all_gather(panel, "row", axis=0, tiled=True)
        return lax.psum_scatter(
            product(local_block, columns), "col", scatter_dimension=0, tiled=True
        )

    second_image = image_of(factor_low[1])
    first_image = image_of(factor_low[0])
    second_solved = right_solve(factor_diag[1], adjoint_low[1] - 2.0 * second_image)
    second_total = lax.psum(product(second_solved.T, factor_low[1]), ("row", "col"))
    second_grad = diag_adjoint(factor_diag[1], adjoint_diag[1] - second_total)
    second_half = 0.5 * second_solved
    upper_term = product(second_half.T, factor_low[0])
    bottom_rows = adjoint_low[0] - 2.0 * (product(second_half, factor_mid) + first_image)
    bottom_solved = right_solve(factor_diag[0], bottom_rows)
    lower_term = product(bottom_solved.T, factor_low[0])
    upper_total = lax.psum(upper_term, ("row", "col"))
    lower_total = lax.psum(lower_term, ("row", "col"))
    top_rows = adjoint_mid - 2.0 * (product(second_grad, factor_mid) + upper_total)
    top_solved = right_solve(factor_diag[0], top_rows)
    first_adjoint = adjoint_diag[0] - product(top_solved.T, factor_mid) - lower_total
    first_grad = diag_adjoint(factor_diag[0], first_adjoint)
    return (
        jnp.stack([first_grad, second_grad]),
        0.5 * top_solved,
        jnp.stack([0.5 * bottom_solved, second_half]),
    )


def solution(mesh):
    return jax.shard_map(
        shards,
        mesh=mesh,
        in_specs=(
            P(),
            P(),
            P(None, ("row", "col"), None),
            P(),
            P(),
            P(None, ("row", "col"), None),
            P("row", None, "col"),
        ),
        out_specs=(P(), P(), P(None, ("row", "col"), None)),
        check_vma=False,
    )
```

profile of v0, /device:TPU:2, one launch (start us, length us, event | category | flops | bytes accessed | tf_op | source)
XLA Modules:
  0.0 587.7 jit_solution(3043104510383694873)
XLA Ops:
  9.8 53.8 %all-gather.5.cloned.1.call-done = f32[1,1024,512]{2,1,0:T(8,128)} async-done(((f32[1,64,512]{2,1,0:T(8,128)}), f32[1,1024,512]{2,1,0:T(8,128)}) %all-gather.5.cloned.1.call-update) | async-done | bytes 2097168 | tf_op jit(solution)/shard_map/all_gather | solution.py:35
  63.6 10.2 %fusion.2 = f32[1024,512]{1,0:T(8,128)} fusion(f32[1024,1024]{0,1:T(8,128)} %bitcast.202, f32[1,1024,512]{2,1,0:T(8,128)} %all-gather.5.cloned.1.call-done), kind=kOutput, calls=%fused_computation.9 | convolution fusion | flops 6442450944 | bytes 8388608 | tf_op jit(solution)/shard_map/dot_general | solution.py:12
  76.9 39.0 %all-gather.7.cloned.1.call-done = f32[1,1024,512]{2,1,0:T(8,128)} async-done(((f32[1,64,512]{2,1,0:T(8,128)}), f32[1,1024,512]{2,1,0:T(8,128)}) %all-gather.7.cloned.1.call-update) | async-done | bytes 2097168 | tf_op jit(solution)/shard_map/all_gather | solution.py:35
  115.9 10.2 %fusion = f32[1024,512]{1,0:T(8,128)} fusion(f32[1024,1024]{0,1:T(8,128)} %bitcast.203, f32[1,1024,512]{2,1,0:T(8,128)} %all-gather.7.cloned.1.call-done), kind=kOutput, calls=%fused_computation.7 | convolution fusion | flops 6442450944 | bytes 8388608 | tf_op jit(solution)/shard_map/dot_general | solution.py:12
  126.4 12.0 %while.14 = (s32[]{:T(128)}, f32[512,512]{1,0:T(8,128)}, s32[4,2]{0,1:T(2,128)S(1)}, f32[4,128,128]{2,1,0:T(8,128)S(1)}, s32[]{:T(128)}) while((s32[]{:T(128)}, f32[512,512]{1,0:T(8,128)}, s32[4,2]{0,1:T(2,128)S(1)}, f32[4,128,128]{2,1,0:T(8,128)S(1)}, s32[]{:T(128)}) %tuple.62), condition=%wide.while_cond.1.clone, body=%wide.while_body.1.clone.sunk | while | flops 2 | bytes 131181 | solution.py:18
  127.1 2.3 bitcast_dynamic-update-slice_fusion.4
  130.1 2.3 bitcast_dynamic-update-slice_fusion.4
  133.1 2.3 bitcast_dynamic-update-slice_fusion.4
  136.2 2.3 bitcast_dynamic-update-slice_fusion.4
  138.5 39.3 %custom-call.17 = f32[4,128,128]{1,2,0:T(8,128)S(1)} custom-call(f32[4,128,128]{2,1,0:T(8,128)S(1)} %get-tuple-element.53), custom_call_target="InvertDiagBlocksLowerTriangular" | custom-call | tf_op jit(solution)/shard_map/jit(_solve_triangular)/triangular_solve | solution.py:18
  177.8 7.7 %while.15 = (s32[]{:T(128)}, f32[512,512]{1,0:T(8,128)S(1)}, s32[4,2]{0,1:T(2,128)S(1)}, f32[4,128,128]{2,1,0:T(8,128)S(1)}, s32[]{:T(128)}) while((s32[]{:T(128)}, f32[512,512]{1,0:T(8,128)S(1)}, s32[4,2]{0,1:T(2,128)S(1)}, f32[4,128,128]{2,1,0:T(8,128)S(1)}, s32[]{:T(128)}) %tuple.80), condition=%wide.while_cond.1.clone.3, body=%wide.while_body.1.clone.3.sunk | while | flops 2 | bytes 131181 | solution.py:18
  186.2 40.1 %custom-call.21 = f32[4,128,128]{1,2,0:T(8,128)S(1)} custom-call(f32[4,128,128]{2,1,0:T(8,128)} %copy-done.21), custom_call_target="InvertDiagBlocksLowerTriangular" | custom-call | tf_op jit(solution)/shard_map/jit(_solve_triangular)/triangular_solve | solution.py:18
  231.7 2.0 fusion.77
  233.8 2.0 fusion.79
  235.8 5.0 reduce-scatter.5.cloned.1.call-done
  244.1 2.0 fusion.75
  247.0 265.8 %all-reduce.3.cloned.1.call-done = (f32[512,512]{1,0:T(8,128)}, f32[512,512]{1,0:T(8,128)}, f32[512,512]{1,0:T(8,128)}) async-done(((f32[512,512]{1,0:T(8,128)}, f32[512,512]{1,0:T(8,128)}, f32[512,512]{1,0:T(8,128)}), (f32[512,512]{1,0:T(8,128)}, f32[512,512]{1,0:T(8,128)}, f32[512,512]{1,0:T(8,128)})) %all-reduce.3.cloned.1.call-update) | async-done | bytes 3145744 | tf_op jit(solution)/shard_map/psum | solution.py:43
  512.8 3.7 convolution_bitcast_fusion.1
  516.5 4.8 gather_fusion
  536.2 3.8 fusion.7
  543.9 2.2 convolution_subtract_fusion.13
  550.9 3.4 fusion.4
  556.2 4.7 gather_fusion.1
  576.9 2.1 multiply_bitcast_fusion.1
  (156 shorter events, 69.4 us)
Async XLA Ops:
  7.2 233.6 %copy-start = (f32[512,512]{1,0:T(8,128)S(1)}, f32[512,512]{1,0:T(8,128)}, u32[]{:S(2)}) copy-start(f32[512,512]{1,0:T(8,128)} %param.12) | copy-start | bytes 3145732
  7.2 56.4 %all-gather.5.cloned.1.call-start = ((), (), s32[]{:S(2)}) async-start(), calls=%async_computation.4 | async-start | bytes 2228224 | tf_op jit(solution)/shard_map/all_gather | solution.py:35
  9.0 106.9 %all-gather.7.cloned.1.call-start = ((), (), s32[]{:S(2)}) async-start(), calls=%async_computation.5 | async-start | bytes 2228224 | tf_op jit(solution)/shard_map/all_gather | solution.py:35
  9.8 216.6 %reduce-scatter.3.cloned.1.call-start = ((), (), s32[]{:S(2)}) async-start(), calls=%async_computation.2 | async-start | bytes 2228224 | tf_op jit(solution)/shard_map/reduce_scatter | solution.py:36
  73.8 1.6 copy-start.1
  73.8 166.9 %reduce-scatter.5.cloned.1.call-start = ((), (), s32[]{:S(2)}) async-start(), calls=%async_computation.3 | async-start | bytes 2228224 | tf_op jit(solution)/shard_map/reduce_scatter | solution.py:36
  126.1 51.7 %copy-start.3 = (f32[512,512]{1,0:T(8,128)S(1)}, f32[512,512]{1,0:T(8,128)}, u32[]{:S(2)}) copy-start(f32[512,512]{1,0:T(8,128)} %get-tuple-element.169) | copy-start | bytes 3145732
  126.1 100.3 %copy-start.20 = (f32[2,64,512]{2,1,0:T(8,128)S(1)}, f32[2,64,512]{2,1,0:T(8,128)}, u32[]{:S(2)}) copy-start(f32[2,64,512]{2,1,0:T(8,128)} %param.16) | copy-start | bytes 786436
  126.1 105.6 %copy-start.19 = (f32[2,64,512]{2,1,0:T(8,128)S(1)}, f32[2,64,512]{2,1,0:T(8,128)}, u32[]{:S(2)}) copy-start(f32[2,64,512]{2,1,0:T(8,128)} %param.13) | copy-start | bytes 786436
  126.2 386.6 %all-reduce.3.cloned.1.call-start = ((), (), s32[]{:S(2)}) async-start(), calls=%async_computation.6 | async-start | bytes 6291456 | tf_op jit(solution)/shard_map/psum | solution.py:43
  177.8 351.5 %copy-start.15 = (f32[4,128,128]{1,2,0:T(8,128)}, f32[4,128,128]{1,2,0:T(8,128)S(1)}, u32[]{:S(2)}) copy-start(f32[4,128,128]{1,2,0:T(8,128)S(1)} %custom-call.17) | copy-start | bytes 786436
  226.3 19.8 %copy-start.6 = (f32[4,128,128]{1,2,0:T(8,128)}, f32[4,128,128]{1,2,0:T(8,128)S(1)}, u32[]{:S(2)}) copy-start(f32[4,128,128]{1,2,0:T(8,128)S(1)} %custom-call.21) | copy-start | bytes 786436
  521.3 1.2 copy-start.5
  531.2 4.9 copy-start.9
  531.4 1.4 copy-start.11
  531.5 1.3 copy-start.12
  532.8 0.7 copy-start.13
  536.2 3.8 copy-start.7
  541.8 1.4 copy-start.14
  548.4 2.6 copy-start.18
  550.9 3.4 copy-start.2
  556.2 4.9 copy-start.8
  561.0 1.2 copy-start.4
  574.4 2.5 copy-start.10
  (3 other events, 2.1 us)
Sparse Core Ops, SparseCore 0:
  11.0 52.5 all-gather.4
  66.6 49.3 all-gather.6
  119.0 60.2 reduce-scatter.2
  181.7 58.9 reduce-scatter.4
  246.9 265.8 all-reduce.2
where the time goes:
time: 594 us; the launch traced here: 588 us
  waiting for transfers between devices  364 us (61%)
  other arithmetic  88.8 us (15%)
  matrix products  72.9 us (12%)
  local copies, waits for them, and re-layouts  46.4 us (8%)
  between operations  14.8 us (2%)
    psum x1, waiting for transfers between devices, shards(): lax.psum(product(second_solved.T, factor_low[1]), ('row', 'col'))  266 us
    all_gather x2, waiting for transfers between devices, image_of(): columns = lax.all_gather(panel, 'row', axis=0, tiled=True)  92.8 us
    another operation x4, other arithmetic, right_solve(): jax.scipy.linalg.solve_triangular(factor, row_block.T, trans=1, lower=True)  81 us
    dot_general x10, matrix products, product(): jnp.dot(left_side, right_side, precision=lax.Precision.HIGHEST, preferred...  41 us
    another operation x36, local copies, waits for them, and re-layouts, right_solve(): jax.scipy.linalg.solve_triangular(factor, row_block.T, trans=1, lower=True)  24.7 us
    another operation x35, matrix products, right_solve(): jax.scipy.linalg.solve_triangular(factor, row_block.T, trans=1, lower=True)  22.8 us
  transfers between devices with their start and end apart: 5, of which 4 were waited for; matrix products, arithmetic and copies ran while one was open for 22% of the time, Pallas kernels for 0%

commit v1 on v0

--- a/solution.py
+++ b/solution.py
@@ -40,7 +40,7 @@
     second_image = image_of(factor_low[1])
     first_image = image_of(factor_low[0])
     second_solved = right_solve(factor_diag[1], adjoint_low[1] - 2.0 * second_image)
-    second_total = lax.psum(product(second_solved.T, factor_low[1]), ("row", "col"))
+    second_total = lax.psum(lax.psum(product(second_solved.T, factor_low[1]), "col"), "row")
     second_grad = diag_adjoint(factor_diag[1], adjoint_diag[1] - second_total)
     second_half = 0.5 * second_solved
     upper_term = product(second_half.T, factor_low[0])

time: 594 us -> 789 us (1.33)
  waiting for transfers between devices: 364 us -> 539 us
  matrix products: 72.9 us -> 89.9 us
    psum x1 -> x3, waiting for transfers between devices: 266 us -> 438 us  [the longest x1 233 us: shards(): lower_total = lax.psum(lower_term, ('row', 'col'))]
    another operation x35, matrix products: 22.8 us -> 37.1 us  [right_solve(): jax.scipy.linalg.solve_triangular(factor, row_block.T, trans=1, lower=True)]
  transfers between devices with their start and end apart: 5 -> 7, of which waited for: 4 -> 6; matrix products, arithmetic and copies ran while one was open for 22% -> 22% of each run, Pallas kernels for 0% -> 0%
where the time goes in v1:
time: 789 us; the launch traced here: 782 us
  waiting for transfers between devices  539 us (68%)
  other arithmetic  92.1 us (12%)
  matrix products  89.9 us (11%)
  local copies, waits for them, and re-layouts  45.1 us (6%)
  between operations  15.1 us (2%)
    psum x1, waiting for transfers between devices, shards(): lower_total = lax.psum(lower_term, ('row', 'col'))  233 us
    psum x1, waiting for transfers between devices, shards(): lax.psum(product(second_solved.T, factor_low[1]), 'col')  110 us
    psum x1, waiting for transfers between devices, shards(): lax.psum(lax.psum(product(second_solved.T, factor_low[1]), 'col'), 'row')  95.3 us
    all_gather x2, waiting for transfers between devices, image_of(): columns = lax.all_gather(panel, 'row', axis=0, tiled=True)  92.7 us
    another operation x4, other arithmetic, right_solve(): jax.scipy.linalg.solve_triangular(factor, row_block.T, trans=1, lower=True)  81.1 us
    dot_general x10, matrix products, product(): jnp.dot(left_side, right_side, precision=lax.Precision.HIGHEST, preferred...  41 us
    another operation x35, matrix products, right_solve(): jax.scipy.linalg.solve_triangular(factor, row_block.T, trans=1, lower=True)  37.1 us
    another operation x36, local copies, waits for them, and re-layouts, right_solve(): jax.scipy.linalg.solve_triangular(factor, row_block.T, trans=1, lower=True)  23.1 us
  transfers between devices with their start and end apart: 7, of which 6 were waited for; matrix products, arithmetic and copies ran while one was open for 22% of the time, Pallas kernels for 0%

profile of v1, /device:TPU:2, one launch (start us, length us, event | category | flops | bytes accessed | tf_op | source)
XLA Modules:
  0.0 781.9 jit_solution(8507142945340313736)
XLA Ops:
  9.8 53.8 %all-gather.5.cloned.1.call-done = f32[1,1024,512]{2,1,0:T(8,128)} async-done(((f32[1,64,512]{2,1,0:T(8,128)}), f32[1,1024,512]{2,1,0:T(8,128)}) %all-gather.5.cloned.1.call-update) | async-done | bytes 2097168 | tf_op jit(solution)/shard_map/all_gather | solution.py:35
  63.6 10.2 %fusion.2 = f32[1024,512]{1,0:T(8,128)} fusion(f32[1024,1024]{0,1:T(8,128)} %bitcast.202, f32[1,1024,512]{2,1,0:T(8,128)} %all-gather.5.cloned.1.call-done), kind=kOutput, calls=%fused_computation.9 | convolution fusion | flops 6442450944 | bytes 8388608 | tf_op jit(solution)/shard_map/dot_general | solution.py:12
  77.0 39.0 %all-gather.7.cloned.1.call-done = f32[1,1024,512]{2,1,0:T(8,128)} async-done(((f32[1,64,512]{2,1,0:T(8,128)}), f32[1,1024,512]{2,1,0:T(8,128)}) %all-gather.7.cloned.1.call-update) | async-done | bytes 2097168 | tf_op jit(solution)/shard_map/all_gather | solution.py:35
  115.9 10.2 %fusion = f32[1024,512]{1,0:T(8,128)} fusion(f32[1024,1024]{0,1:T(8,128)} %bitcast.203, f32[1,1024,512]{2,1,0:T(8,128)} %all-gather.7.cloned.1.call-done), kind=kOutput, calls=%fused_computation.7 | convolution fusion | flops 6442450944 | bytes 8388608 | tf_op jit(solution)/shard_map/dot_general | solution.py:12
  126.4 11.7 %while.14 = (s32[]{:T(128)}, f32[512,512]{1,0:T(8,128)}, s32[4,2]{0,1:T(2,128)S(1)}, f32[4,128,128]{2,1,0:T(8,128)S(1)}, s32[]{:T(128)}) while((s32[]{:T(128)}, f32[512,512]{1,0:T(8,128)}, s32[4,2]{0,1:T(2,128)S(1)}, f32[4,128,128]{2,1,0:T(8,128)S(1)}, s32[]{:T(128)}) %tuple.60), condition=%wide.while_cond.1.clone, body=%wide.while_body.1.clone.sunk | while | flops 2 | bytes 131189 | solution.py:18
  130.0 2.3 bitcast_dynamic-update-slice_fusion.4
  133.0 2.3 bitcast_dynamic-update-slice_fusion.4
  138.2 39.3 %custom-call.17 = f32[4,128,128]{1,2,0:T(8,128)S(1)} custom-call(f32[4,128,128]{2,1,0:T(8,128)S(1)} %get-tuple-element.53), custom_call_target="InvertDiagBlocksLowerTriangular" | custom-call | tf_op jit(solution)/shard_map/jit(_solve_triangular)/triangular_solve | solution.py:18
  177.5 8.0 %while.15 = (s32[]{:T(128)}, f32[512,512]{1,0:T(8,128)S(1)}, s32[4,2]{0,1:T(2,128)S(1)}, f32[4,128,128]{2,1,0:T(8,128)S(1)}, s32[]{:T(128)}) while((s32[]{:T(128)}, f32[512,512]{1,0:T(8,128)S(1)}, s32[4,2]{0,1:T(2,128)S(1)}, f32[4,128,128]{2,1,0:T(8,128)S(1)}, s32[]{:T(128)}) %tuple.82), condition=%wide.while_cond.1.clone.3, body=%wide.while_body.1.clone.3.sunk | while | flops 2 | bytes 131189 | solution.py:18
  186.2 40.1 %custom-call.21 = f32[4,128,128]{1,2,0:T(8,128)S(1)} custom-call(f32[4,128,128]{2,1,0:T(8,128)} %copy-done.22), custom_call_target="InvertDiagBlocksLowerTriangular" | custom-call | tf_op jit(solution)/shard_map/jit(_solve_triangular)/triangular_solve | solution.py:18
  233.7 7.0 reduce-scatter.5.cloned.1.call-done
  244.0 110.4 %all-reduce.5.cloned.1.call-done = f32[512,512]{1,0:T(8,128)} async-done(((f32[512,512]{1,0:T(8,128)}), f32[512,512]{1,0:T(8,128)}) %all-reduce.5.cloned.1.call-update) | async-done | bytes 1048592 | tf_op jit(solution)/shard_map/psum | solution.py:43
  359.6 95.3 %all-reduce.7.cloned.1.call-done = f32[512,512]{1,0:T(8,128)} async-done(((f32[512,512]{1,0:T(8,128)}), f32[512,512]{1,0:T(8,128)}) %all-reduce.7.cloned.1.call-update) | async-done | bytes 1048592 | tf_op jit(solution)/shard_map/psum | solution.py:43
  454.8 3.7 convolution_bitcast_fusion.1
  458.6 4.8 gather_fusion
  468.8 2.4 convolution_subtract_fusion.15
  482.3 2.8 convolution_subtract_fusion.14
  489.7 2.4 fusion.162
  492.0 232.8 %all-reduce.9.cloned.1.call-done = (f32[512,512]{1,0:T(8,128)}, f32[512,512]{1,0:T(8,128)}) async-done(((f32[512,512]{1,0:T(8,128)}, f32[512,512]{1,0:T(8,128)}), (f32[512,512]{1,0:T(8,128)}, f32[512,512]{1,0:T(8,128)})) %all-reduce.9.cloned.1.call-update) | async-done | bytes 2097168 | tf_op jit(solution)/shard_map/psum | solution.py:51
  724.8 3.9 fusion.7
  735.7 3.1 convolution_subtract_fusion.13
  742.5 3.4 fusion.4
  747.8 4.7 gather_fusion.1
  764.0 3.1 convolution_subtract_fusion.11
  (166 shorter events, 89.8 us)
Async XLA Ops:
  7.2 233.6 %copy-start = (f32[512,512]{1,0:T(8,128)S(1)}, f32[512,512]{1,0:T(8,128)}, u32[]{:S(2)}) copy-start(f32[512,512]{1,0:T(8,128)} %param.12) | copy-start | bytes 3145732
  7.2 56.4 %all-gather.5.cloned.1.call-start = ((), (), s32[]{:S(2)}) async-start(), calls=%async_computation.6 | async-start | bytes 2228224 | tf_op jit(solution)/shard_map/all_gather | solution.py:35
  9.0 106.9 %all-gather.7.cloned.1.call-start = ((), (), s32[]{:S(2)}) async-start(), calls=%async_computation.7 | async-start | bytes 2228224 | tf_op jit(solution)/shard_map/all_gather | solution.py:35
  9.8 216.7 %reduce-scatter.3.cloned.1.call-start = ((), (), s32[]{:S(2)}) async-start(), calls=%async_computation.2 | async-start | bytes 2228224 | tf_op jit(solution)/shard_map/reduce_scatter | solution.py:36
  73.8 1.6 copy-start.1
  73.8 167.0 %reduce-scatter.5.cloned.1.call-start = ((), (), s32[]{:S(2)}) async-start(), calls=%async_computation.5 | async-start | bytes 2228224 | tf_op jit(solution)/shard_map/reduce_scatter | solution.py:36
  126.1 51.4 %copy-start.3 = (f32[512,512]{1,0:T(8,128)S(1)}, f32[512,512]{1,0:T(8,128)}, u32[]{:S(2)}) copy-start(f32[512,512]{1,0:T(8,128)} %get-tuple-element.164) | copy-start | bytes 3145732
  126.1 100.3 %copy-start.21 = (f32[2,64,512]{2,1,0:T(8,128)S(1)}, f32[2,64,512]{2,1,0:T(8,128)}, u32[]{:S(2)}) copy-start(f32[2,64,512]{2,1,0:T(8,128)} %param.16) | copy-start | bytes 786436
  126.1 105.6 %copy-start.20 = (f32[2,64,512]{2,1,0:T(8,128)S(1)}, f32[2,64,512]{2,1,0:T(8,128)}, u32[]{:S(2)}) copy-start(f32[2,64,512]{2,1,0:T(8,128)} %param.13) | copy-start | bytes 786436
  126.1 228.3 %all-reduce.5.cloned.1.call-start = ((), (), s32[]{:S(2)}) async-start(), calls=%async_computation.3 | async-start | bytes 2097152 | tf_op jit(solution)/shard_map/psum | solution.py:43
  177.5 65.0 %copy-start.12 = (f32[4,128,128]{1,2,0:T(8,128)}, f32[4,128,128]{1,2,0:T(8,128)S(1)}, u32[]{:S(2)}) copy-start(f32[4,128,128]{1,2,0:T(8,128)S(1)} %custom-call.17) | copy-start | bytes 786436
  243.2 211.6 %all-reduce.7.cloned.1.call-start = ((), (), s32[]{:S(2)}) async-start(), calls=%async_computation.4 | async-start | bytes 2097152 | tf_op jit(solution)/shard_map/psum | solution.py:43
  354.4 370.4 %all-reduce.9.cloned.1.call-start = ((), (), s32[]{:S(2)}) async-start(), calls=%async_computation.8 | async-start | bytes 4194304 | tf_op jit(solution)/shard_map/psum | solution.py:51
  474.1 12.2 %copy-start.6 = (f32[128,512]{0,1:T(8,128)}, f32[128,512]{0,1:T(8,128)S(1)}, u32[]{:S(2)}) copy-start(f32[128,512]{0,1:T(8,128)S(1)} %copy.28) | copy-start | bytes 786436
  477.0 2.3 copy-start.11
  477.2 9.2 %copy-start.7 = (f32[128,512]{0,1:T(8,128)}, f32[128,512]{0,1:T(8,128)S(1)}, u32[]{:S(2)}) copy-start(f32[128,512]{0,1:T(8,128)S(1)} %copy.27) | copy-start | bytes 786436
  482.3 4.0 copy-start.8
  738.8 3.6 copy-start.16
  739.0 3.5 copy-start.19
  742.5 3.4 copy-start.2
  757.3 1.0 copy-start.5
  758.8 9.9 %copy-start.14 = (f32[128,512]{0,1:T(8,128)}, f32[128,512]{0,1:T(8,128)S(1)}, u32[]{:S(2)}) copy-start(f32[128,512]{0,1:T(8,128)S(1)} %copy.37) | copy-start | bytes 786436
  767.3 1.5 copy-start.17
  771.4 1.5 copy-start.4
  (6 other events, 5.0 us)
Sparse Core Ops, SparseCore 0:
  11.0 52.5 all-gather.4
  66.6 49.3 all-gather.6
  119.0 60.2 reduce-scatter.2
  181.7 59.0 reduce-scatter.4
  243.5 110.8 all-reduce.4
  357.5 97.2 all-reduce.6
  460.4 264.3 all-reduce.8
